TPU v7x, 256 devices: a whole 4x4x8 slice. The times are simulated.
256 devices in a mesh: seq: 64 (over x, z, core), head: 4 (over y).
Axes of the slice: x: 4, y: 4, z: 8, core: 2. Of those that a mesh axis runs over, the one named last changes fastest.
Arguments:
- tokens: bfloat16 [65536, 2048], P('seq', 'head'), may hold values from -6 to 6
- w_qkv: bfloat16 [2048, 6144], P(None, 'head'), may hold values from -1 to 1
- item_at: int32 [4, 2048], P('head'), may hold values from 0 to 2047, as said below
- rand_cols: int32 [16, 512, 4], P('head'), may hold values from 0 to 511, as said below
- rand_used: int32 [16, 512], P('head'), may hold values from 0 to 4, as said below
Outputs:
- attended: bfloat16 [4, 2048, 128, 128], P('head', 'seq')
Inputs may be any that keep to these rules, and one draw needn't show every extreme that they name: In head group g, item e * 512 + r stands for head g * 4 + e at block row r, and every item appears exactly once in item_at[g]. Positions j * 32 to (j + 1) * 32 - 1 hold the items placed at device j of seq. Of the items whose block rows lie on one device of seq, at most 1 of one group are placed at any one device, and exactly 1 at some. `rand_cols`: take all 128 candidates (used or not) of the items placed at one device in one head group, or of the items of one group whose block rows lie on one device: at most 2 of them lie in the block rows of any one device of seq, and exactly 2 in some. A candidate may equal a window block or block 0. `rand_used`: in each head group the counts of the 32 items placed at one device sum to exactly 64; the sums over the items whose block rows lie on one device vary.
All inputs are finite; a program needn't handle non-finite values.
Results may differ from a plain program's by a relative error of at most 0.019.
Values may be sent and summed in bfloat16 or wider, within the bound.
No kernel may reach another device: no remote copies, remote signals or barrier semaphores. Data moves between devices by JAX's collectives and lax.ppermute only.
A program may use at most 128 MiB of HBM per device.

v0:
```python
import math
import jax
import jax.numpy as jnp
from jax import lax
from jax.sharding import PartitionSpec as P

neg_large = -1e30


def extended(block, sides, width):
    for axis, dim in sides:
        count = lax.axis_size(axis)
        forward = [(i, i + 1) for i in range(count - 1)]
        backward = [(target, source) for source, target in forward]
        low = lax.ppermute(
            lax.slice_in_dim(block, block.shape[dim] - width, None, axis=dim), axis, forward
        )
        high = lax.ppermute(lax.slice_in_dim(block, 0, width, axis=dim), axis, backward)
        block = jnp.concatenate([low, block, high], axis=dim)
    return block


def broadcast(block, axis, owner):
    block = jnp.where(lax.axis_index(axis) == owner, block, jnp.zeros_like(block))
    return lax.psum(block, axis)


def packed_attend(
    queries, near_keys, near_values, near_usable, rand_keys, rand_values, slot_item, factor
):
    item_count = queries.shape[0]
    near_scores = (
        jnp.einsum("ibe,ijke->ibjk", queries, near_keys, preferred_element_type=jnp.float32)
        * factor
    )
    near_scores = jnp.where(near_usable[:, None, :, None], near_scores, neg_large)
    rand_scores = (
        jnp.einsum(
            "kbe,kce->kbc", queries[slot_item], rand_keys, preferred_element_type=jnp.float32
        )
        * factor
    )
    member = slot_item[None, :] == jnp.arange(item_count, dtype=jnp.int32)[:, None]
    slot_max = jnp.max(rand_scores, axis=2)
    rand_max = jnp.max(jnp.where(member[:, :, None], slot_max[None], neg_large), axis=1)
    row_max = jnp.maximum(jnp.max(near_scores, axis=(2, 3)), rand_max)
    near_expo = jnp.exp(near_scores - row_max[:, :, None, None])
    rand_expo = jnp.exp(rand_scores - row_max[slot_item][:, :, None])
    slot_total = jnp.sum(rand_expo, axis=2)
    row_sum = jnp.sum(near_expo, axis=(2, 3)) + jnp.sum(
        jnp.where(member[:, :, None], slot_total[None], 0.0), axis=1
    )
    summed = jnp.einsum(
        "ibjk,ijke->ibe",
        near_expo.astype(jnp.bfloat16),
        near_values,
        preferred_element_type=jnp.float32,
    )
    slot_out = jnp.einsum(
        "kbc,kce->kbe",
        rand_expo.astype(jnp.bfloat16),
        rand_values,
        preferred_element_type=jnp.float32,
    )
    summed = summed + jnp.einsum(
        "ik,kbe->ibe", member.astype(jnp.float32), slot_out, precision=lax.Precision.HIGHEST
    )
    return (summed, row_max, row_sum)


def rank_among(homes):
    count = homes.shape[-1]
    earlier = jnp.tril(jnp.ones((count, count), bool), -1)
    same_home = homes[..., :, None] == homes[..., None, :]
    return jnp.sum(same_home & earlier, axis=-1)


def pack_live(counts, rand_count, live_total):
    slot_total = counts.shape[0] * rand_count
    slot_ids = jnp.arange(slot_total, dtype=jnp.int32)
    live = slot_ids % rand_count < jnp.repeat(counts, rand_count)
    live_rank = jnp.cumsum(live.astype(jnp.int32)) - 1
    picks = live[:, None] & (live_rank[:, None] == jnp.arange(live_total, dtype=jnp.int32)[None, :])
    return jnp.sum(jnp.where(picks, slot_ids[:, None], 0), axis=0)


def local(tokens, w_qkv, item_at, rand_cols, rand_used):
    seq_count = lax.axis_size("seq")
    my_seq = lax.axis_index("seq")
    heads_dev, nblocks, rand_count = rand_cols.shape
    tokens_dev = tokens.shape[0]
    head_dim = w_qkv.shape[1] // (3 * heads_dev)
    block_len = tokens_dev * seq_count // nblocks
    rows_dev = tokens_dev // block_len
    items_dev = heads_dev * rows_dev
    slot_count = items_dev * rand_count
    live_total = slot_count // 2
    cap_items = max(1, items_dev // seq_count)
    cap_tiles = max(1, slot_count // seq_count)
    factor = 1.0 / math.sqrt(head_dim)
    projected = jnp.dot(
        lax.all_gather(tokens, "head", axis=1, tiled=True),
        w_qkv,
        preferred_element_type=jnp.float32,
    )
    projected = projected.astype(jnp.bfloat16).reshape(rows_dev, block_len, 3, heads_dev, head_dim)
    query_tiles = projected[:, :, 0].transpose(2, 0, 1, 3).reshape(items_dev, block_len, head_dim)
    pair_rows = projected[:, :, 1:].reshape(tokens_dev, 2, heads_dev, head_dim)
    widened = extended(pair_rows, (("seq", 0),), block_len)
    pair_tiles = widened.reshape(rows_dev + 2, block_len, 2, heads_dev, head_dim).transpose(
        3, 0, 2, 1, 4
    )
    own_tiles = pair_tiles[:, 1 : rows_dev + 1].reshape(items_dev, 2, block_len, head_dim)
    first_tiles = broadcast(pair_tiles[:, 1], "seq", 0)
    window_tiles = jnp.stack(
        [
            pair_tiles[:, 0:rows_dev],
            pair_tiles[:, 1 : rows_dev + 1],
            pair_tiles[:, 2 : rows_dev + 2],
        ],
        axis=2,
    )
    window_tiles = window_tiles.reshape(items_dev, 3, 2, block_len, head_dim)
    placed = item_at[0].reshape(seq_count, items_dev)
    placed_head = placed // nblocks
    placed_row = placed % nblocks
    placed_home = placed_row // rows_dev
    local_index = placed_head * rows_dev + placed_row % rows_dev
    is_mine = placed_home == my_seq
    rank_mine = jnp.cumsum(is_mine.astype(jnp.int32), axis=1) - 1
    slot_ids = jnp.arange(cap_items, dtype=jnp.int32)
    slot_hit = is_mine[:, :, None] & (rank_mine[:, :, None] == slot_ids)
    send_index = jnp.sum(jnp.where(slot_hit, local_index[:, :, None], 0), axis=1).reshape(-1)
    my_items = lax.dynamic_index_in_dim(placed, my_seq, 0, keepdims=False)
    item_head = my_items // nblocks
    item_row = my_items % nblocks
    item_home = item_row // rows_dev
    recv_slot = item_home * cap_items + rank_among(item_home)
    my_random = rand_cols[item_head, item_row].reshape(-1)
    tile_home = my_random // rows_dev
    tile_rank = rank_among(tile_home)
    tile_slot = tile_home * cap_tiles + tile_rank
    tile_ids = jnp.arange(cap_tiles, dtype=jnp.int32)
    peer_ids = jnp.arange(seq_count, dtype=jnp.int32)
    slot_head = jnp.repeat(item_head, rand_count)
    tile_local = slot_head * rows_dev + my_random % rows_dev
    wanted = (tile_home[None, :, None] == peer_ids[:, None, None]) & (
        tile_rank[None, :, None] == tile_ids[None, None, :]
    )
    requests = jnp.sum(jnp.where(wanted, tile_local[None, :, None], 0), axis=1)
    asked = lax.all_to_all(requests, "seq", split_axis=0, concat_axis=0, tiled=True)
    picked = own_tiles[asked.reshape(-1)].reshape(asked.shape + own_tiles.shape[1:])
    fetched = lax.all_to_all(picked, "seq", split_axis=0, concat_axis=0, tiled=True)
    gathered = fetched.reshape(seq_count * cap_tiles, 2, block_len, head_dim)[tile_slot]
    random_tiles = gathered.reshape(items_dev, rand_count, 2, block_len, head_dim)
    item_counts = rand_used[item_head, item_row]
    live_slots = pack_live(item_counts, rand_count, live_total)
    packed_tiles = random_tiles.reshape(slot_count, 2, block_len, head_dim)[live_slots]
    slot_item = live_slots // rand_count
    global_tiles = first_tiles[item_head][:, None]
    sent_query = query_tiles[send_index].reshape(seq_count, cap_items, block_len, head_dim)
    sent_window = window_tiles[send_index].reshape(seq_count, cap_items, 3, 2, block_len, head_dim)
    got_query, got_window = (
        lax.all_to_all(sent_query, "seq", split_axis=0, concat_axis=0, tiled=True),
        lax.all_to_all(sent_window, "seq", split_axis=0, concat_axis=0, tiled=True),
    )
    queries = got_query.reshape(seq_count * cap_items, block_len, head_dim)[recv_slot]
    windows = got_window.reshape(seq_count * cap_items, 3, 2, block_len, head_dim)[recv_slot]
    near_tiles = jnp.concatenate([windows, global_tiles], axis=1)
    near_usable = jnp.concatenate(
        [
            (item_row >= 1)[:, None],
            jnp.ones((items_dev, 1), bool),
            (item_row + 1 < nblocks)[:, None],
            jnp.ones((items_dev, 1), bool),
        ],
        axis=1,
    )
    summed, row_max, row_sum = packed_attend(
        queries,
        near_tiles[:, :, 0],
        near_tiles[:, :, 1],
        near_usable,
        packed_tiles[:, 0],
        packed_tiles[:, 1],
        slot_item,
        factor,
    )
    result = (summed / row_sum[:, :, None]).astype(jnp.bfloat16)
    return result.reshape(1, items_dev, block_len, head_dim)


def solution(mesh):
    return jax.shard_map(
        local,
        mesh=mesh,
        in_specs=(
            P("seq", "head"),
            P(None, "head"),
            P("head", None),
            P("head", None, None),
            P("head", None),
        ),
        out_specs=P("head", "seq", None, None),
        check_vma=False,
    )
```

profile of v0, /device:TPU:1, one launch (start us, length us, event | category | flops | bytes accessed | tf_op | source)
XLA Modules:
  0.0 679.1 jit_solution(8968216010016144075)
XLA Ops:
  13.3 13.0 %all-to-all-start.2 = ((s32[64,1,2]{2,1,0:T(1,128)}), s32[64,1,2]{2,1,0:T(1,128)S(1)}, u32[]{:S(2)}, u32[]{:S(2)}) async-start(s32[64,1,2]{2,1,0:T(1,128)} %copy.118), calls=%async_computation.2 | async-start | bytes 65536 | tf_op jit(solution)/shard_map/all_to_all | solution.py:151
  27.5 36.4 %all-gather.2.cloned.1.call-done = bf16[1024,2048]{1,0:T(8,128)(2,1)} async-done(((bf16[1024,512]{1,0:T(8,128)(2,1)}), bf16[1024,2048]{1,0:T(8,128)(2,1)}) %all-gather.2.cloned.1.call-update) | async-done | bytes 4194320 | tf_op jit(solution)/shard_map/all_gather | solution.py:102
  63.8 11.2 %convolution_convert_fusion = bf16[1024,1536]{1,0:T(8,128)(2,1)} fusion(bf16[1024,2048]{1,0:T(8,128)(2,1)} %all-gather.2.cloned.1.call-done, bf16[2048,1536]{1,0:T(8,128)(2,1)} %param.6), kind=kOutput, calls=%fused_computation.35 | convolution fusion | flops 6444023808 | bytes 13631488 | tf_op jit(solution)/shard_map/dot_general | solution.py:101
  75.0 5.0 reshape.931
  81.6 3.3 gather_fusion
  85.0 10.9 %all-to-all-start = ((bf16[64,1,128,128]{3,2,1,0:T(8,128)(2,1)}), bf16[64,1,128,128]{3,2,1,0:T(8,128)(2,1)}, u32[]{:S(2)}, u32[]{:S(2)}) async-start(bf16[64,1,128,128]{3,2,1,0:T(8,128)(2,1)} %bitcast.166), calls=%async_computation | async-start | bytes 4194304 | tf_op jit(solution)/shard_map/all_to_all | solution.py:164
  96.8 3.5 collective-permute-start
  101.1 2.1 collective-permute-start.1
  105.3 38.3 %collective-permute-done = bf16[128,2,4,128]{3,0,2,1:T(8,128)(2,1)S(1)} collective-permute-done((bf16[128,2,4,128]{3,0,2,1:T(8,128)(2,1)}, bf16[128,2,4,128]{3,0,2,1:T(8,128)(2,1)S(1)}, u32[]{:S(2)}, u32[]{:S(2)}) %collective-permute-start) | collective-permute-done | bytes 262176 | tf_op jit(solution)/shard_map/ppermute | solution.py:15
  143.6 2.4 collective-permute-done.1
  147.5 3.7 fusion.86
  151.4 6.7 gather_fusion.8
  158.0 9.3 %all-to-all-start.3 = ((bf16[64,2,2,128,128]{4,3,2,1,0:T(8,128)(2,1)}), bf16[64,2,2,128,128]{4,3,2,1,0:T(8,128)(2,1)}, u32[]{:S(2)}, u32[]{:S(2)}) async-start(bf16[64,2,2,128,128]{4,3,2,1,0:T(8,128)(2,1)} %bitcast.161), calls=%async_computation.3 | async-start | bytes 16777216 | tf_op jit(solution)/shard_map/all_to_all | solution.py:153
  167.4 1.9 copy.109
  169.8 3.3 pad_maximum_fusion
  173.1 10.0 %gather_fusion.2 = bf16[64,3,2,128,128]{4,3,2,1,0:T(8,128)(2,1)} fusion(bf16[32,3,2,128,128]{4,3,2,0,1:T(8,128)(2,1)} %pad_maximum_fusion, s32[1024]{0:T(1024)S(1)} %pad_clamp_fusion.6), kind=kCustom, calls=%fused_computation.2 | custom fusion | bytes 25166080 | tf_op jit(solution)/shard_map/gather | solution.py:162
  183.1 170.1 %all-to-all-done.3 = bf16[64,2,2,128,128]{4,3,2,1,0:T(8,128)(2,1)} async-done(((bf16[64,2,2,128,128]{4,3,2,1,0:T(8,128)(2,1)}), bf16[64,2,2,128,128]{4,3,2,1,0:T(8,128)(2,1)}, u32[]{:S(2)}, u32[]{:S(2)}) %all-to-all-start.3) | async-done | bytes 8388640 | tf_op jit(solution)/shard_map/all_to_all | solution.py:153
  353.1 6.2 all-to-all-start.1
  363.3 221.0 %all-reduce.2.cloned.1.call-done = bf16[4,2,128,128]{3,2,1,0:T(8,128)(2,1)} async-done(((bf16[4,2,128,128]{3,2,1,0:T(8,128)(2,1)}), bf16[4,2,128,128]{3,2,1,0:T(8,128)(2,1)}) %all-reduce.2.cloned.1.call-update) | async-done | bytes 262160 | tf_op jit(solution)/shard_map/psum | solution.py:25
  584.3 1.9 gather_fusion.4
  587.7 2.3 gather_fusion.1
  591.0 10.0 %gather_fusion.9 = bf16[128,2,128,128]{3,2,1,0:T(8,128)(2,1)} fusion(bf16[128,2,128,128]{3,2,1,0:T(8,128)(2,1)} %bitcast.37, s32[1024]{0:T(1024)S(1)} %pad_clamp_fusion.1), kind=kCustom, calls=%fused_computation.9 | custom fusion | bytes 16777728 | tf_op jit(solution)/shard_map/gather | solution.py:154
  601.0 6.4 gather_fusion.10
  607.4 5.2 multiply_reduce_fusion
  613.1 25.2 %all-to-all-done.1 = bf16[64,1,3,2,128,128]{5,4,3,2,1,0:T(8,128)(2,1)} async-done(((bf16[64,1,3,2,128,128]{5,4,3,2,1,0:T(8,128)(2,1)}), bf16[64,1,3,2,128,128]{5,4,3,2,1,0:T(8,128)(2,1)}, u32[]{:S(2)}, u32[]{:S(2)}) %all-to-all-start.1) | async-done | bytes 12582944 | tf_op jit(solution)/shard_map/all_to_all | solution.py:165
  638.3 8.7 %gather_fusion.3 = bf16[32,3,2,128,128]{4,3,2,1,0:T(8,128)(2,1)} fusion(bf16[64,3,2,128,128]{4,3,2,1,0:T(8,128)(2,1)} %bitcast.26, s32[1024]{0:T(1024)S(1)} %pad_clamp_fusion.5), kind=kCustom, calls=%fused_computation.3 | custom fusion | bytes 12583040 | tf_op jit(solution)/shard_map/gather | solution.py:168
  647.0 5.5 fusion
  653.1 3.3 fusion.18
  656.6 2.7 fusion.20
  660.6 2.1 fusion.1
  662.7 4.1 fusion.12
  666.8 5.5 fusion.31
  (100 shorter events, 24.1 us)
Async XLA Ops:
  6.5 353.1 %copy-start = (s32[4,512]{1,0:T(4,128)S(1)}, s32[4,512]{1,0:T(4,128)}, u32[]{:S(2)}) copy-start(s32[4,512]{1,0:T(4,128)} %param.9) | copy-start | bytes 24580
  6.5 57.3 %all-gather.2.cloned.1.call-start = ((), (), s32[]{:S(2)}) async-start(), calls=%async_computation.4 | async-start | bytes 5242880 | tf_op jit(solution)/shard_map/all_gather | solution.py:102
  13.3 71.7 %all-to-all-start.2 = ((s32[64,1,2]{2,1,0:T(1,128)}), s32[64,1,2]{2,1,0:T(1,128)S(1)}, u32[]{:S(2)}, u32[]{:S(2)}) async-start(s32[64,1,2]{2,1,0:T(1,128)} %copy.118), calls=%async_computation.2 | async-start | bytes 65536 | tf_op jit(solution)/shard_map/all_to_all | solution.py:151
  85.0 73.1 %all-to-all-start = ((bf16[64,1,128,128]{3,2,1,0:T(8,128)(2,1)}), bf16[64,1,128,128]{3,2,1,0:T(8,128)(2,1)}, u32[]{:S(2)}, u32[]{:S(2)}) async-start(bf16[64,1,128,128]{3,2,1,0:T(8,128)(2,1)} %bitcast.166), calls=%async_computation | async-start | bytes 4194304 | tf_op jit(solution)/shard_map/all_to_all | solution.py:164
  96.8 46.8 %collective-permute-start = (bf16[128,2,4,128]{3,0,2,1:T(8,128)(2,1)}, bf16[128,2,4,128]{3,0,2,1:T(8,128)(2,1)S(1)}, u32[]{:S(2)}, u32[]{:S(2)}) collective-permute-start(bf16[128,2,4,128]{3,0,2,1:T(8,128)(2,1)} %bitcast.157), channel_id=1, source_target_pairs={{0,4},{4,8},{8,12},{12,16},{16,20},{20,24},{24,28},{28,32},{32,36}... | collective-permute-start | bytes 786440 | tf_op jit(solution)/shard_map/ppermute | solution.py:15
  101.1 44.9 %collective-permute-start.1 = (bf16[128,2,4,128]{3,0,2,1:T(8,128)(2,1)}, bf16[128,2,4,128]{3,0,2,1:T(8,128)(2,1)}, u32[]{:S(2)}, u32[]{:S(2)}) collective-permute-start(bf16[128,2,4,128]{3,0,2,1:T(8,128)(2,1)} %bitcast.156), channel_id=1, source_target_pairs={{4,0},{8,4},{12,8},{16,12},{20,16},{24,20},{28,24},{32,28},{36,32}... | collective-permute-start | bytes 786440 | tf_op jit(solution)/shard_map/ppermute | solution.py:18
  147.5 3.8 copy-start.3
  158.0 195.1 %all-to-all-start.3 = ((bf16[64,2,2,128,128]{4,3,2,1,0:T(8,128)(2,1)}), bf16[64,2,2,128,128]{4,3,2,1,0:T(8,128)(2,1)}, u32[]{:S(2)}, u32[]{:S(2)}) async-start(bf16[64,2,2,128,128]{4,3,2,1,0:T(8,128)(2,1)} %bitcast.161), calls=%async_computation.3 | async-start | bytes 16777216 | tf_op jit(solution)/shard_map/all_to_all | solution.py:153
  167.3 2.2 copy-start.5
  353.1 7.9 %copy-start.7 = (s32[32]{0:T(128)S(1)}, s32[32]{0:T(128)}, u32[]{:S(2)}) copy-start(s32[32]{0:T(128)} %get-tuple-element.21) | copy-start | bytes 388
  353.1 285.1 %all-to-all-start.1 = ((bf16[64,1,3,2,128,128]{5,4,3,2,1,0:T(8,128)(2,1)}), bf16[64,1,3,2,128,128]{5,4,3,2,1,0:T(8,128)(2,1)}, u32[]{:S(2)}, u32[]{:S(2)}) async-start(bf16[64,1,3,2,128,128]{5,4,3,2,1,0:T(8,128)(2,1)} %bitcast.160), calls=%async_computation.1 | async-start | bytes 25165824 | tf_op jit(solution)/shard_map/all_to_all | solution.py:165
  359.3 225.0 %all-reduce.2.cloned.1.call-start = ((), (), s32[]{:S(2)}) async-start(), calls=%async_computation.5 | async-start | bytes 524288 | tf_op jit(solution)/shard_map/psum | solution.py:25
  638.3 8.7 %copy-start.6 = (bf16[32,2,128,128]{3,2,0,1:T(8,128)(2,1)S(1)}, bf16[32,2,128,128]{3,2,0,1:T(8,128)(2,1)}, u32[]{:S(2)}) copy-start(bf16[32,2,128,128]{3,2,0,1:T(8,128)(2,1)} %copy.158) | copy-start | bytes 6291460
  653.1 3.4 copy-start.2
  656.6 4.0 copy-start.4
  656.6 10.2 %slice-start = ((s8[6291456]{0:T(1024)(128)(4,1)}), s8[4194304]{0:T(1024)(128)(4,1)S(1)}, s32[]{:S(2)}) async-start(s8[6291456]{0:T(1024)(128)(4,1)} %bitcast.170), calls=%async_computation.6 | async-start | bytes 8388608
  660.6 6.2 slice-start.1
  666.8 5.5 copy-start.1
Sparse Core Ops, SparseCore 0:
  9.2 54.5 all-gather.1
  363.6 220.6 all-reduce.1
where the time goes:
time: 680 us; the launch traced here: 679 us
  waiting for transfers between devices  494 us (73%)
  local copies, waits for them, and re-layouts  75.2 us (11%)
  starting transfers between devices  45.3 us (7%)
  matrix products  34.2 us (5%)
  other arithmetic  16.5 us (2%)
  between operations  13.8 us (2%)
    psum x1, waiting for transfers between devices, broadcast(): return lax.psum(block, axis)  221 us
    all_to_all x1, waiting for transfers between devices, local(): lax.all_to_all(picked, 'seq', split_axis=0, concat_axis=0, tiled=True)  170 us
    ppermute x1, waiting for transfers between devices, extended(): lax.ppermute(lax.slice_in_dim(block, block.shape[dim] - width, None, axis...  38.3 us
    all_gather x1, waiting for transfers between devices, local(): lax.all_gather(tokens, 'head', axis=1, tiled=True)  36.4 us
    all_to_all x1, waiting for transfers between devices, local(): lax.all_to_all(sent_window, 'seq', split_axis=0, concat_axis=0, tiled=True)  25.2 us
  transfers between devices with their start and end apart: 8, of which 6 were waited for; matrix products, arithmetic and copies ran while one was open for 14% of the time, Pallas kernels for 0%

commit v1 on v0

--- a/solution.py
+++ b/solution.py
@@ -3,6 +3,7 @@
 import jax.numpy as jnp
 from jax import lax
 from jax.sharding import PartitionSpec as P
+from jax.lax import all_gather
 
 neg_large = -1e30
 
@@ -22,7 +23,7 @@
 
 def broadcast(block, axis, owner):
     block = jnp.where(lax.axis_index(axis) == owner, block, jnp.zeros_like(block))
-    return lax.psum(block, axis)
+    return jnp.sum(all_gather(block, axis), axis=0)
 
 
 def packed_attend(

time: 680 us -> 734 us (1.079)
  waiting for transfers between devices: 494 us -> 544 us
    all_to_all x1, waiting for transfers between devices: 25.2 us -> 248 us  [local(): lax.all_to_all(sent_window, 'seq', split_axis=0, concat_axis=0, tiled=True)]
    psum x1 -> x0, waiting for transfers between devices: 221 us -> none  [broadcast(): return lax.psum(block, axis)]
    all_to_all x1, waiting for transfers between devices: 170 us -> 217 us  [local(): lax.all_to_all(picked, 'seq', split_axis=0, concat_axis=0, tiled=True)]
  transfers between devices with their start and end apart: 8 -> 8, of which waited for: 6 -> 5; matrix products, arithmetic and copies ran while one was open for 14% -> 13% of each run, Pallas kernels for 0% -> 0%
where the time goes in v1:
time: 734 us; the launch traced here: 733 us
  waiting for transfers between devices  544 us (74%)
  local copies, waits for them, and re-layouts  72.6 us (10%)
  starting transfers between devices  44.9 us (6%)
  matrix products  34.7 us (5%)
  other arithmetic  22.6 us (3%)
  between operations  13.9 us (2%)
    all_to_all x1, waiting for transfers between devices, local(): lax.all_to_all(sent_window, 'seq', split_axis=0, concat_axis=0, tiled=True)  248 us
    all_to_all x1, waiting for transfers between devices, local(): lax.all_to_all(picked, 'seq', split_axis=0, concat_axis=0, tiled=True)  217 us
    ppermute x1, waiting for transfers between devices, extended(): lax.ppermute(lax.slice_in_dim(block, block.shape[dim] - width, None, axis...  38.3 us
    all_gather x1, waiting for transfers between devices, local(): lax.all_gather(tokens, 'head', axis=1, tiled=True)  37 us
  transfers between devices with their start and end apart: 8, of which 5 were waited for; matrix products, arithmetic and copies ran while one was open for 13% of the time, Pallas kernels for 0%

profile of v1, /device:TPU:1, one launch (start us, length us, event | category | flops | bytes accessed | tf_op | source)
XLA Modules:
  0.0 733.1 jit_solution(1563439440185042986)
XLA Ops:
  12.6 13.0 %all-to-all-start.2 = ((s32[64,1,2]{2,1,0:T(1,128)}), s32[64,1,2]{2,1,0:T(1,128)S(1)}, u32[]{:S(2)}, u32[]{:S(2)}) async-start(s32[64,1,2]{2,1,0:T(1,128)} %copy.113), calls=%async_computation.2 | async-start | bytes 65536 | tf_op jit(solution)/shard_map/all_to_all | solution.py:152
  26.8 37.0 %all-gather.4.cloned.1.call-done = bf16[1024,2048]{1,0:T(8,128)(2,1)} async-done(((bf16[1024,512]{1,0:T(8,128)(2,1)}), bf16[1024,2048]{1,0:T(8,128)(2,1)}) %all-gather.4.cloned.1.call-update) | async-done | bytes 4194320 | tf_op jit(solution)/shard_map/all_gather | solution.py:103
  63.8 11.2 %convolution_convert_fusion = bf16[1024,1536]{1,0:T(8,128)(2,1)} fusion(bf16[1024,2048]{1,0:T(8,128)(2,1)} %all-gather.4.cloned.1.call-done, bf16[2048,1536]{1,0:T(8,128)(2,1)} %param.6), kind=kOutput, calls=%fused_computation.36 | convolution fusion | flops 6444023808 | bytes 13631488 | tf_op jit(solution)/shard_map/dot_general | solution.py:102
  75.0 5.0 reshape.941
  81.6 3.4 gather_fusion
  85.0 10.9 %all-to-all-start = ((bf16[64,1,128,128]{3,2,1,0:T(8,128)(2,1)}), bf16[64,1,128,128]{3,2,1,0:T(8,128)(2,1)}, u32[]{:S(2)}, u32[]{:S(2)}) async-start(bf16[64,1,128,128]{3,2,1,0:T(8,128)(2,1)} %bitcast.166), calls=%async_computation | async-start | bytes 4194304 | tf_op jit(solution)/shard_map/all_to_all | solution.py:165
  96.8 3.5 collective-permute-start
  101.1 2.1 collective-permute-start.1
  105.3 38.3 %collective-permute-done = bf16[128,2,4,128]{3,0,2,1:T(8,128)(2,1)S(1)} collective-permute-done((bf16[128,2,4,128]{3,0,2,1:T(8,128)(2,1)}, bf16[128,2,4,128]{3,0,2,1:T(8,128)(2,1)S(1)}, u32[]{:S(2)}, u32[]{:S(2)}) %collective-permute-start) | collective-permute-done | bytes 262176 | tf_op jit(solution)/shard_map/ppermute | solution.py:16
  143.6 2.4 collective-permute-done.1
  147.2 3.8 fusion.85
  151.1 6.7 gather_fusion.8
  157.8 9.3 %all-to-all-start.3 = ((bf16[64,2,2,128,128]{4,3,2,1,0:T(8,128)(2,1)}), bf16[64,2,2,128,128]{4,3,2,1,0:T(8,128)(2,1)}, u32[]{:S(2)}, u32[]{:S(2)}) async-start(bf16[64,2,2,128,128]{4,3,2,1,0:T(8,128)(2,1)} %bitcast.161), calls=%async_computation.3 | async-start | bytes 16777216 | tf_op jit(solution)/shard_map/all_to_all | solution.py:154
  167.2 1.7 slice_select_fusion
  168.9 1.9 copy.103
  171.3 3.1 pad_maximum_fusion
  174.5 10.1 %gather_fusion.2 = bf16[64,3,2,128,128]{4,3,2,1,0:T(8,128)(2,1)} fusion(bf16[32,3,2,128,128]{4,3,2,0,1:T(8,128)(2,1)} %pad_maximum_fusion, s32[1024]{0:T(1024)S(1)} %pad_clamp_fusion.6), kind=kCustom, calls=%fused_computation.2 | custom fusion | bytes 25166080 | tf_op jit(solution)/shard_map/gather | solution.py:163
  184.6 217.4 %all-to-all-done.3 = bf16[64,2,2,128,128]{4,3,2,1,0:T(8,128)(2,1)} async-done(((bf16[64,2,2,128,128]{4,3,2,1,0:T(8,128)(2,1)}), bf16[64,2,2,128,128]{4,3,2,1,0:T(8,128)(2,1)}, u32[]{:S(2)}, u32[]{:S(2)}) %all-to-all-start.3) | async-done | bytes 8388640 | tf_op jit(solution)/shard_map/all_to_all | solution.py:154
  402.0 6.1 all-to-all-start.1
  410.2 2.3 gather_fusion.1
  413.5 9.9 %gather_fusion.9 = bf16[128,2,128,128]{3,2,1,0:T(8,128)(2,1)} fusion(bf16[128,2,128,128]{3,2,1,0:T(8,128)(2,1)} %bitcast.38, s32[1024]{0:T(1024)S(1)} %pad_clamp_fusion.1), kind=kCustom, calls=%fused_computation.9 | custom fusion | bytes 16777728 | tf_op jit(solution)/shard_map/gather | solution.py:155
  423.4 6.4 gather_fusion.10
  429.8 5.2 multiply_reduce_fusion
  435.3 248.5 %all-to-all-done.1 = bf16[64,1,3,2,128,128]{5,4,3,2,1,0:T(8,128)(2,1)} async-done(((bf16[64,1,3,2,128,128]{5,4,3,2,1,0:T(8,128)(2,1)}), bf16[64,1,3,2,128,128]{5,4,3,2,1,0:T(8,128)(2,1)}, u32[]{:S(2)}, u32[]{:S(2)}) %all-to-all-start.1) | async-done | bytes 12582944 | tf_op jit(solution)/shard_map/all_to_all | solution.py:166
  683.8 8.6 %gather_fusion.3 = bf16[32,3,2,128,128]{4,3,2,1,0:T(8,128)(2,1)} fusion(bf16[64,3,2,128,128]{4,3,2,1,0:T(8,128)(2,1)} %bitcast.27, s32[1024]{0:T(1024)S(1)} %pad_clamp_fusion.5), kind=kCustom, calls=%fused_computation.3 | custom fusion | bytes 12583040 | tf_op jit(solution)/shard_map/gather | solution.py:169
  692.4 6.8 bitcast_reduce_fusion
  700.4 6.2 fusion
  707.2 3.3 fusion.18
  710.6 2.7 fusion.20
  714.6 2.1 fusion.1
  716.7 4.1 fusion.12
  720.9 5.4 fusion.31
  (105 shorter events, 20.9 us)
Async XLA Ops:
  6.5 401.7 %copy-start = (s32[4,512]{1,0:T(4,128)S(1)}, s32[4,512]{1,0:T(4,128)}, u32[]{:S(2)}) copy-start(s32[4,512]{1,0:T(4,128)} %param.9) | copy-start | bytes 24580
  6.5 57.3 %all-gather.4.cloned.1.call-start = ((), (), s32[]{:S(2)}) async-start(), calls=%async_computation.4 | async-start | bytes 5242880 | tf_op jit(solution)/shard_map/all_gather | solution.py:103
  10.3 1.1 copy-start.8
  12.6 72.4 %all-to-all-start.2 = ((s32[64,1,2]{2,1,0:T(1,128)}), s32[64,1,2]{2,1,0:T(1,128)S(1)}, u32[]{:S(2)}, u32[]{:S(2)}) async-start(s32[64,1,2]{2,1,0:T(1,128)} %copy.113), calls=%async_computation.2 | async-start | bytes 65536 | tf_op jit(solution)/shard_map/all_to_all | solution.py:152
  85.0 72.8 %all-to-all-start = ((bf16[64,1,128,128]{3,2,1,0:T(8,128)(2,1)}), bf16[64,1,128,128]{3,2,1,0:T(8,128)(2,1)}, u32[]{:S(2)}, u32[]{:S(2)}) async-start(bf16[64,1,128,128]{3,2,1,0:T(8,128)(2,1)} %bitcast.166), calls=%async_computation | async-start | bytes 4194304 | tf_op jit(solution)/shard_map/all_to_all | solution.py:165
  96.8 46.8 %collective-permute-start = (bf16[128,2,4,128]{3,0,2,1:T(8,128)(2,1)}, bf16[128,2,4,128]{3,0,2,1:T(8,128)(2,1)S(1)}, u32[]{:S(2)}, u32[]{:S(2)}) collective-permute-start(bf16[128,2,4,128]{3,0,2,1:T(8,128)(2,1)} %bitcast.156), channel_id=1, source_target_pairs={{0,4},{4,8},{8,12},{12,16},{16,20},{20,24},{24,28},{28,32},{32,36}... | collective-permute-start | bytes 786440 | tf_op jit(solution)/shard_map/ppermute | solution.py:16
  101.1 44.9 %collective-permute-start.1 = (bf16[128,2,4,128]{3,0,2,1:T(8,128)(2,1)}, bf16[128,2,4,128]{3,0,2,1:T(8,128)(2,1)}, u32[]{:S(2)}, u32[]{:S(2)}) collective-permute-start(bf16[128,2,4,128]{3,0,2,1:T(8,128)(2,1)} %bitcast.155), channel_id=1, source_target_pairs={{4,0},{8,4},{12,8},{16,12},{20,16},{24,20},{28,24},{32,28},{36,32}... | collective-permute-start | bytes 786440 | tf_op jit(solution)/shard_map/ppermute | solution.py:19
  147.2 3.8 copy-start.3
  157.8 244.3 %all-to-all-start.3 = ((bf16[64,2,2,128,128]{4,3,2,1,0:T(8,128)(2,1)}), bf16[64,2,2,128,128]{4,3,2,1,0:T(8,128)(2,1)}, u32[]{:S(2)}, u32[]{:S(2)}) async-start(bf16[64,2,2,128,128]{4,3,2,1,0:T(8,128)(2,1)} %bitcast.161), calls=%async_computation.3 | async-start | bytes 16777216 | tf_op jit(solution)/shard_map/all_to_all | solution.py:154
  167.1 525.3 %all-gather.6.cloned.1.call-start = ((), (), s32[]{:S(2)}) async-start(), calls=%async_computation.5 | async-start | bytes 17039360 | tf_op jit(solution)/shard_map/all_gather | solution.py:26
  168.9 2.2 copy-start.5
  402.0 7.2 copy-start.9
  402.0 281.8 %all-to-all-start.1 = ((bf16[64,1,3,2,128,128]{5,4,3,2,1,0:T(8,128)(2,1)}), bf16[64,1,3,2,128,128]{5,4,3,2,1,0:T(8,128)(2,1)}, u32[]{:S(2)}, u32[]{:S(2)}) async-start(bf16[64,1,3,2,128,128]{5,4,3,2,1,0:T(8,128)(2,1)} %bitcast.160), calls=%async_computation.1 | async-start | bytes 25165824 | tf_op jit(solution)/shard_map/all_to_all | solution.py:166
  700.4 6.2 copy-start.6
  707.1 3.4 copy-start.2
  710.6 4.0 copy-start.4
  710.6 10.2 %slice-start = ((s8[6291456]{0:T(1024)(128)(4,1)}), s8[4194304]{0:T(1024)(128)(4,1)S(1)}, s32[]{:S(2)}) async-start(s8[6291456]{0:T(1024)(128)(4,1)} %bitcast.170), calls=%async_computation.6 | async-start | bytes 8388608
  714.6 6.2 slice-start.1
  716.7 4.1 copy-start.7
  720.9 5.4 copy-start.1
Sparse Core Ops, SparseCore 0:
  9.2 54.5 all-gather.3
  170.8 216.8 all-gather.5
